TPU v7x, 32 devices: a whole 2x2x4 slice. The times are simulated.
32 devices in a mesh: grp: 2 (over y), seq: 4 (over z), usr: 4 (over x, core).
Axes of the slice: x: 2, y: 2, z: 4, core: 2. Of those that a mesh axis runs over, the one named last changes fastest.
Arguments:
- history_kv: bfloat16 [16, 2048, 768], P(('grp', 'usr'), 'seq'), parts along dimension 0, may hold values from -6 to 6
- candidates: bfloat16 [16, 512, 768], P(('grp', 'usr'), 'seq'), parts along dimension 0, may hold values from -6 to 6
- lengths: int32 [16], P(('grp', 'usr')), parts along dimension 0, may hold values from 256 to 2048, as said below
- w_query: bfloat16 [768, 384], replicated, may hold values from -0.21875 to 0.21875
- w_gate: bfloat16 [768, 384], replicated, may hold values from -0.21875 to 0.21875
- token_mix: bfloat16 [512, 512], P('seq'), may hold values from -0.25 to 0.25
- w_out: bfloat16 [384, 768], replicated, may hold values from -0.3125 to 0.3125
- w_up: bfloat16 [768, 2048], P(None, 'usr'), may hold values from -0.21875 to 0.21875
- w_down: bfloat16 [2048, 768], P('usr'), may hold values from -0.125 to 0.125
Outputs:
- ranked: bfloat16 [16, 512, 768], P(('grp', 'usr'), 'seq'), parts along dimension 0
There are 2 independent parts, one for each index of `grp`. A program takes and returns all parts, laid end to end along the dimension named above; an argument that names none is the same for every part. Nothing has to cross between parts.
Inputs may be any that keep to these rules, and one draw needn't show every extreme that they name: lengths[u] counts the first valid slots of user u's history; in every draw one user has exactly 2048 and another exactly 256.
All inputs are finite; a program needn't handle non-finite values.
Results may differ from a plain program's by a relative error of at most 0.008.
Values may be sent and summed in bfloat16 or wider, within the bound.
A program may use at most 64 MiB of HBM per device.

v0:
```python
import math

import jax
import jax.numpy as jnp
from jax import lax
from jax.sharding import PartitionSpec as P

HEADS = 3
DH = 128


def layer_norm(values):
    center = values - jnp.mean(values, axis=-1, keepdims=True)
    spread = jnp.mean(center * center, axis=-1, keepdims=True)
    return center * lax.rsqrt(spread + 1e-05)


def shards(history_kv, candidates, lengths, w_query, w_gate, token_mix, w_out, w_up, w_down):
    user_count, hist_dev, _ = history_kv.shape
    inner = w_query.shape[1]
    half = hist_dev // 2
    scale = 1.0 / math.sqrt(DH)
    seq_index = lax.axis_index("seq")
    first_start = seq_index * hist_dev
    sections = ((history_kv[:, :half], first_start), (history_kv[:, half:], first_start + half))
    offsets = lax.iota(jnp.int32, half)
    queries = jnp.einsum(
        "ucd,de->uce", candidates, w_query, preferred_element_type=jnp.float32
    ).astype(jnp.bfloat16)
    piece = lax.all_gather(queries, "seq", axis=1, tiled=True)
    row_count = piece.shape[1]
    results = []
    for member in range(user_count):
        query_heads = piece[member].reshape(row_count, HEADS, DH)
        limit = lengths[member]
        summed = jnp.zeros((row_count, inner), jnp.float32)
        for section, section_start in sections:
            key_heads = section[member, :, :inner].reshape(half, HEADS, DH)
            value_heads = section[member, :, inner:].reshape(half, HEADS, DH)

            def compute(
                operand,
                key_heads=key_heads,
                value_heads=value_heads,
                section_start=section_start,
                query_heads=query_heads,
                limit=limit,
            ):
                scores = (
                    jnp.einsum(
                        "chd,thd->hct", query_heads, key_heads, preferred_element_type=jnp.float32
                    )
                    * scale
                )
                visible = section_start + offsets < limit
                weights = jnp.where(visible[None, None, :], jax.nn.silu(scores), 0.0).astype(
                    jnp.bfloat16
                )
                contrib = jnp.einsum(
                    "hct,thd->chd", weights, value_heads, preferred_element_type=jnp.float32
                )
                return contrib.reshape(row_count, inner)

            def skipped(operand):
                return jnp.zeros((row_count, inner), jnp.float32)

            summed = summed + lax.cond(section_start < limit, compute, skipped, 0)
        results.append(summed)
    partial_sums = jnp.stack(results)
    attended = lax.psum_scatter(partial_sums, "seq", scatter_dimension=1, tiled=True)
    normed = layer_norm(attended).astype(jnp.bfloat16)
    mixed = normed.astype(jnp.float32) + jnp.einsum(
        "cp,upe->uce",
        token_mix,
        lax.all_gather(normed, "seq", axis=1, tiled=True),
        preferred_element_type=jnp.float32,
    )
    gate_values = jax.nn.silu(
        jnp.einsum("ucd,de->uce", candidates, w_gate, preferred_element_type=jnp.float32)
    )
    gated = (mixed * gate_values).astype(jnp.bfloat16)
    state = candidates.astype(jnp.float32) + jnp.einsum(
        "uce,ed->ucd", gated, w_out, preferred_element_type=jnp.float32
    )
    ffn_in = layer_norm(state).astype(jnp.bfloat16)
    hidden = jax.nn.gelu(
        jnp.einsum(
            "ucd,df->ucf",
            lax.all_gather(ffn_in, "usr", axis=0, tiled=True),
            w_up,
            preferred_element_type=jnp.float32,
        )
    ).astype(jnp.bfloat16)
    ffn_terms = jnp.einsum("ucf,fd->ucd", hidden, w_down, preferred_element_type=jnp.float32)
    ffn_out = lax.psum_scatter(
        ffn_terms.astype(jnp.bfloat16), "usr", scatter_dimension=0, tiled=True
    ).astype(jnp.float32)
    return (state + ffn_out).astype(jnp.bfloat16)


def solution(mesh):
    return jax.shard_map(
        shards,
        mesh=mesh,
        in_specs=(
            P(("grp", "usr"), "seq", None),
            P(("grp", "usr"), "seq", None),
            P(("grp", "usr")),
            P(),
            P(),
            P("seq", None),
            P(),
            P(None, "usr"),
            P("usr", None),
        ),
        out_specs=P(("grp", "usr"), "seq", None),
        check_vma=False,
    )
```

profile of v0, /device:TPU:0, one launch (start us, length us, event | category | flops | bytes accessed | tf_op | source)
XLA Modules:
  0.0 179.6 jit_solution(5376608440595050645)
XLA Ops:
  10.3 1.6 convolution_convert_fusion.1
  11.8 21.3 %all_gather.9 = bf16[2,512,384]{2,1,0:T(8,128)(2,1)S(1)} all-gather(bf16[2,128,384]{2,1,0:T(8,128)(2,1)S(1)} %convolution_convert_fusion.1), channel_id=1, replica_groups=mesh['grp'=2,'seq'=4,'usr'=4] {'seq'}, dimensions={1}, use_global_device_ids=true | all-gather | bytes 983040 | tf_op jit(solution)/shard_map/all_gather | solution.py:30
  34.7 6.5 %conditional.5 = (f32[512,384]{0,1:T(8,128)S(1)}) conditional(s32[]{:T(128)} %convert_element_type.57, () %tuple.31, (s32[]{:T(128)}, s32[256]{0:T(256)S(1)}, s32[]{:T(128)}, bf16[2,512,768]{2,1,0:T(8,128)(2,1)S(1)}, bf16[512,3,128]{0,2,1:T(8,128)(2,1)}) %tuple.77), branch_computations={%region_2.3_spmd, %region_3.4_spmd} | conditional | flops 204079616 | bytes 5506576 | solution.py:67
  34.7 1.6 copy.47
  36.3 1.8 fusion.65
  39.3 1.9 %fusion.8 = f32[3,512,128]{1,2,0:T(8,128)S(1)} fusion(bf16[256,3,128]{0,2,1:T(8,128)(2,1)} %bitcast.89, bf16[512,3,128]{0,2,1:T(8,128)(2,1)} %get-tuple-element.146, bf16[256,3,128]{0,2,1:T(8,128)(2,1)} %bitcast.88, pred[256]{0:T(512)(128)(4,1)} %add_compare_fusion.1), kind=kOutput, calls=%fused_computation.11 | convolution fusion | flops 204079104 | bytes 1573120 | tf_op jit(solution)/shard_map/cond/branch_1_fun/hct,thd->chd/dot_general | solution.py:59
  41.2 6.7 %conditional.7 = (f32[512,384]{0,1:T(8,128)}) conditional(s32[]{:T(128)} %convert_element_type.59, () %tuple.35, (s32[]{:T(128)}, s32[256]{0:T(256)S(1)}, s32[]{:T(128)}, bf16[2,512,768]{2,1,0:T(8,128)(2,1)S(1)}, bf16[512,3,128]{0,2,1:T(8,128)(2,1)S(1)}) %tuple.75), branch_computations={%region_6.7_spmd, %region_7.8_spmd} | conditional | flops 204079616 | bytes 5506576 | solution.py:67
  41.2 1.6 copy.52
  42.9 1.8 fusion.67
  45.2 2.7 %fusion.24 = f32[3,512,128]{1,2,0:T(8,128)} fusion(bf16[256,3,128]{0,2,1:T(8,128)(2,1)} %bitcast.91, bf16[512,3,128]{0,2,1:T(8,128)(2,1)S(1)} %get-tuple-element.156, bf16[256,3,128]{0,2,1:T(8,128)(2,1)} %bitcast.90, pred[256]{0:T(512)(128)(4,1)S(1)} %add_compare_fusion.3), kind=kOutput, calls=%fused_computation.31 | convolution fusion | flops 204079104 | bytes 1573120 | tf_op jit(solution)/shard_map/cond/branch_1_fun/hct,thd->chd/dot_general | solution.py:59
  47.9 6.9 %conditional.4 = (f32[512,384]{0,1:T(8,128)}) conditional(s32[]{:T(128)} %convert_element_type.55, () %tuple.29, (s32[]{:T(128)}, s32[256]{0:T(256)S(1)}, s32[]{:T(128)}, bf16[2,512,768]{2,1,0:T(8,128)(2,1)S(1)}, bf16[512,3,128]{0,2,1:T(8,128)(2,1)}) %tuple.78), branch_computations={%region_0.0_spmd, %region_1.2_spmd} | conditional | flops 204079616 | bytes 5506576 | solution.py:67
  47.9 1.6 copy.45
  49.5 1.8 %fusion.64 = (bf16[1,256,384]{1,2,0:T(8,128)(2,1)}, bf16[1,256,384]{1,2,0:T(8,128)(2,1)}) fusion(bf16[2,512,768]{1,2,0:T(8,128)(2,1)} %copy.45), kind=kLoop, calls=%fused_computation.87 | loop fusion | bytes 786432 | tf_op jit(solution)/shard_map/slice | solution.py:38
  52.0 2.8 %fusion = f32[3,512,128]{1,2,0:T(8,128)} fusion(bf16[256,3,128]{0,2,1:T(8,128)(2,1)} %bitcast.93, bf16[512,3,128]{0,2,1:T(8,128)(2,1)} %get-tuple-element.141, bf16[256,3,128]{0,2,1:T(8,128)(2,1)} %bitcast.92, pred[256]{0:T(512)(128)(4,1)S(1)} %add_compare_fusion), kind=kOutput, calls=%fused_computation.1 | convolution fusion | flops 204079104 | bytes 1573120 | tf_op jit(solution)/shard_map/cond/branch_1_fun/hct,thd->chd/dot_general | solution.py:59
  54.8 4.0 %conditional.6 = (f32[512,384]{0,1:T(8,128)S(1)}) conditional(s32[]{:T(128)} %convert_element_type.58, () %tuple.33, (s32[]{:T(128)}, s32[256]{0:T(256)S(1)}, s32[]{:T(128)}, bf16[2,512,768]{2,1,0:T(8,128)(2,1)S(1)}, bf16[512,3,128]{0,2,1:T(8,128)(2,1)S(1)}) %tuple.76), branch_computations={%region_4.5_spmd, %region_5.6_spmd} | conditional | flops 204079616 | bytes 5506576 | solution.py:67
  54.8 1.6 copy.50
  58.8 1.7 add_bitcast_fusion
  63.4 32.3 %reduce-scatter.3.cloned.1.call-done = f32[2,128,384]{1,2,0:T(8,128)} async-done(((f32[2,512,384]{1,2,0:T(8,128)}), f32[2,128,384]{1,2,0:T(8,128)}) %reduce-scatter.3.cloned.1.call-update) | async-done | bytes 393232 | tf_op jit(solution)/shard_map/reduce_scatter | solution.py:70
  98.9 17.2 %all_gather.10 = bf16[2,512,384]{1,2,0:T(8,128)(2,1)S(1)} all-gather(bf16[2,128,384]{1,2,0:T(8,128)(2,1)S(1)} %multiply_convert_fusion.1), channel_id=1, replica_groups=mesh['grp'=2,'seq'=4,'usr'=4] {'seq'}, dimensions={1}, use_global_device_ids=true | all-gather | bytes 983040 | tf_op jit(solution)/shard_map/all_gather | solution.py:75
  116.0 2.0 %fusion.70 = (f32[2,128]{1,0:T(2,128)S(1)}, f32[2,128,768]{2,1,0:T(8,128)S(1)}) fusion(bf16[384,768]{1,0:T(8,128)(2,1)} %param.23, bf16[2,512,384]{1,2,0:T(8,128)(2,1)S(1)} %all_gather.10, f32[2,128,384]{1,2,0:T(8,128)S(1)} %fusion.47, bf16[2,128,384]{1,2,0:T(8,128)(2,1)S(1)} %multiply_convert_fusion.1, bf16[128,512]{1,0:T(8,128)(2,1)S(1)} %copy-done.5, ...), kind=kOutput, calls=%fused_computation.93 | convolution fusion | flops 253034240 | bytes 3277824 | tf_op jit(solution)/shard_map/uce,ed->ucd/dot_general | solution.py:82
  119.3 19.3 %all-gather.2.cloned.1.call-done = bf16[8,128,768]{2,1,0:T(8,128)(2,1)} async-done(((bf16[2,128,768]{2,1,0:T(8,128)(2,1)}), bf16[8,128,768]{2,1,0:T(8,128)(2,1)}) %all-gather.2.cloned.1.call-update) | async-done | bytes 1572880 | tf_op jit(solution)/shard_map/all_gather | solution.py:89
  138.5 4.6 %convolution_convert_fusion = bf16[8,128,768]{2,1,0:T(8,128)(2,1)} fusion(bf16[8,128,768]{2,1,0:T(8,128)(2,1)} %all-gather.2.cloned.1.call-done, bf16[512,768]{1,0:T(8,128)(2,1)S(1)} %copy-done, bf16[768,512]{1,0:T(8,128)(2,1)S(1)} %copy-done.4), kind=kOutput, calls=%fused_computation.49 | convolution fusion | flops 1616117760 | bytes 4718592 | tf_op jit(solution)/shard_map/ucf,fd->ucd/dot_general | solution.py:94
  143.1 28.1 %reduce-scatter.5.cloned.1.call-done = bf16[2,128,768]{2,1,0:T(8,128)(2,1)} async-done(((bf16[8,128,768]{2,1,0:T(8,128)(2,1)}), bf16[2,128,768]{2,1,0:T(8,128)(2,1)}) %reduce-scatter.5.cloned.1.call-update) | async-done | bytes 393232 | tf_op jit(solution)/shard_map/reduce_scatter | solution.py:95
  171.3 1.8 %add_convert_fusion = bf16[2,128,768]{2,1,0:T(8,128)(2,1)} fusion(f32[2,128,768]{2,1,0:T(8,128)S(1)} %get-tuple-element.170, bf16[2,128,768]{2,1,0:T(8,128)(2,1)} %reduce-scatter.5.cloned.1.call-done), kind=kLoop, calls=%fused_computation.59 | loop fusion | flops 589824 | bytes 1572864 | tf_op jit(solution)/shard_map/convert_element_type | solution.py:98
  (43 shorter events, 14.9 us)
Async XLA Ops:
  6.5 132.0 %copy-start = (bf16[512,768]{1,0:T(8,128)(2,1)S(1)}, bf16[512,768]{1,0:T(8,128)(2,1)}, u32[]{:S(2)}) copy-start(bf16[512,768]{1,0:T(8,128)(2,1)} %param.25) | copy-start | bytes 2359300
  6.5 89.1 %reduce-scatter.3.cloned.1.call-start = ((), (), s32[]{:S(2)}) async-start(), calls=%async_computation.2 | async-start | bytes 1966080 | tf_op jit(solution)/shard_map/reduce_scatter | solution.py:70
  33.1 1.6 copy-start.1
  61.9 1.0 copy-start.2
  61.9 1.2 copy-start.3
  61.9 54.2 %copy-start.5 = (bf16[128,512]{1,0:T(8,128)(2,1)S(1)}, bf16[128,512]{1,0:T(8,128)(2,1)}, u32[]{:S(2)}) copy-start(bf16[128,512]{1,0:T(8,128)(2,1)} %param.22) | copy-start | bytes 393220
  61.9 76.6 %all-gather.2.cloned.1.call-start = ((), (), s32[]{:S(2)}) async-start(), calls=%async_computation.3 | async-start | bytes 1966080 | tf_op jit(solution)/shard_map/all_gather | solution.py:89
  118.0 20.5 %copy-start.4 = (bf16[768,512]{1,0:T(8,128)(2,1)S(1)}, bf16[768,512]{1,0:T(8,128)(2,1)}, u32[]{:S(2)}) copy-start(bf16[768,512]{1,0:T(8,128)(2,1)} %param.24) | copy-start | bytes 2359300
  119.2 52.1 %reduce-scatter.5.cloned.1.call-start = ((), (), s32[]{:S(2)}) async-start(), calls=%async_computation.4 | async-start | bytes 1966080 | tf_op jit(solution)/shard_map/reduce_scatter | solution.py:95
Sparse Core Ops, SparseCore 0:
  62.0 33.6 reduce-scatter.2
  119.3 19.1 all-gather.1
  143.2 27.9 reduce-scatter.4
where the time goes:
time: 180 us
  waiting for transfers between devices  79.7 us (44%)
  blocking collectives  38.5 us (21%)
  local copies, waits for them, and re-layouts  16.8 us (9%)
  matrix products  16.7 us (9%)
  between operations  15.6 us (9%)
  other arithmetic  12.2 us (7%)
    reduce_scatter x1, waiting for transfers between devices, shards(): lax.psum_scatter(partial_sums, 'seq', scatter_dimension=1, tiled=True)  32.3 us
    reduce_scatter x1, waiting for transfers between devices, shards(): lax.psum_scatter(ffn_terms.astype(jnp.bfloat16), 'usr', scatter_dimension...  28.1 us
    all_gather x1, blocking collectives, shards(): piece = lax.all_gather(queries, 'seq', axis=1, tiled=True)  21.3 us
    all_gather x1, waiting for transfers between devices, shards(): lax.all_gather(ffn_in, 'usr', axis=0, tiled=True)  19.3 us
    all_gather x1, blocking collectives, shards(): lax.all_gather(normed, 'seq', axis=1, tiled=True)  17.2 us
    dot_general x4, matrix products, compute(): jnp.einsum('hct,thd->chd', weights, value_heads, preferred_element_type=j...  8.25 us
    another operation x4, local copies, waits for them, and re-layouts  6.43 us
    slice x4, local copies, waits for them, and re-layouts, shards(): key_heads = section[member, :, :inner].reshape(half, HEADS, DH)  6.42 us
  transfers between devices with their start and end apart: 3, of which 3 were waited for; matrix products, arithmetic and copies ran while one was open for 0% of the time, Pallas kernels for 0%

commit v1 on v0

--- a/solution.py
+++ b/solution.py
@@ -1,18 +1,347 @@
+import functools
 import math
 
 import jax
 import jax.numpy as jnp
 from jax import lax
+from jax.experimental import pallas as pl
+from jax.experimental.pallas import tpu as pltpu
 from jax.sharding import PartitionSpec as P
 
 HEADS = 3
 DH = 128
+F32 = jnp.float32
+BF16 = jnp.bfloat16
+MESH = pl.DeviceIdType.MESH
 
 
 def layer_norm(values):
     center = values - jnp.mean(values, axis=-1, keepdims=True)
     spread = jnp.mean(center * center, axis=-1, keepdims=True)
     return center * lax.rsqrt(spread + 1e-05)
+
+
+def silu_of_double(half):
+    return half + half * jnp.tanh(half)
+
+
+def gelu_tanh(v):
+    return 0.5 * v * (1.0 + jnp.tanh(math.sqrt(2.0 / math.pi) * (v + 0.044715 * (v * v * v))))
+
+
+def dot(a, b):
+    return jnp.dot(a, b, preferred_element_type=F32)
+
+
+def kernel(
+    seqs,
+    kv_hbm, cand_hbm, len_ref, wq_hbm, wg_hbm, tm_hbm, wo_hbm, wu_hbm, wd_hbm,
+    out_ref,
+    kv, cand, wq, wg, tm, wo, wu, wd,
+    values, queries, sums, outgoing, incoming, normed, gates, states,
+    load_sem,
+    q_send, q_recv, p_send, p_recv, n_send, n_recv,
+    wc_send, wc_recv, wx_send, wx_recv, wy_send, wy_recv,
+):
+    users, rows, _ = cand.shape
+    hist = kv.shape[1]
+    inner = wq.shape[1]
+    hidden_slots = wu.shape[0]
+    g, s, u = lax.axis_index("grp"), lax.axis_index("seq"), lax.axis_index("usr")
+    partner = u + 1 - 2 * lax.rem(u, 2)
+    across = lax.rem(u + 2, 4)
+    across_partner = lax.rem(partner + 2, 4)
+    left, right = (g, s - 1, u), (g, s + 1, u)
+    has_left, has_right = s > 0, s < seqs - 1
+
+    loads = {}
+    for index, (name, source, target) in enumerate((
+        ("cand", cand_hbm, cand), ("wq", wq_hbm, wq), ("kv", kv_hbm, kv), ("wg", wg_hbm, wg),
+        ("tm", tm_hbm, tm), ("wo", wo_hbm, wo), ("wu", wu_hbm, wu.at[u]), ("wd", wd_hbm, wd.at[u]),
+    )):
+        loads[name] = pltpu.make_async_copy(source, target, load_sem.at[index])
+        loads[name].start()
+
+    barrier = pltpu.get_barrier_semaphore()
+    for peer in ((g, s, partner), (g, s, across), (1 - g, s, u)):
+        pl.semaphore_signal(barrier, inc=1, device_id=peer, device_id_type=MESH)
+
+    @pl.when(has_left)
+    def _():
+        pl.semaphore_signal(barrier, inc=1, device_id=left, device_id_type=MESH)
+
+    @pl.when(has_right)
+    def _():
+        pl.semaphore_signal(barrier, inc=1, device_id=right, device_id_type=MESH)
+
+    def remote(source, target, send, recv, device):
+        return pltpu.make_async_remote_copy(
+            src_ref=source, dst_ref=target, send_sem=send, recv_sem=recv,
+            device_id=device, device_id_type=MESH,
+        )
+
+    weights = ((wu_hbm, wu), (wd_hbm, wd))
+
+    def half_of(w, slot, half):
+        size = weights[w][1].shape[1] // 2
+        return weights[w][1].at[slot, pl.ds(pl.multiple_of(half * size, size), size)]
+
+    def own_half(w, half):
+        size = weights[w][1].shape[1] // 2
+        return weights[w][0].at[pl.ds(pl.multiple_of(half * size, size), size)]
+
+    def to_partner_own(w, slot):
+        return remote(weights[w][0], weights[w][1].at[slot], wc_send.at[w, 0], wc_recv.at[w, 0], (g, s, partner))
+
+    def to_across(w, slot):
+        return remote(own_half(w, g), half_of(w, slot, g), wx_send.at[w], wx_recv.at[w], (g, s, across))
+
+    def to_group(w, half):
+        part = half_of(w, across, half)
+        return remote(part, part, wy_send.at[w], wy_recv.at[w], (1 - g, s, u))
+
+    def to_partner_far(w, slot, half, which):
+        part = half_of(w, slot, half)
+        return remote(part, part, wc_send.at[w, which], wc_recv.at[w, which], (g, s, partner))
+
+    def across_arrived(w):
+        to_across(w, across).wait_recv()
+        to_group(w, g).start()
+        to_partner_far(w, across, g, 1).start()
+
+    def group_arrived(w):
+        to_group(w, 1 - g).wait_recv()
+        to_partner_far(w, across, 1 - g, 2).start()
+
+    def gather_copy(buf, send, recv, m, block, way):
+        ref = buf.at[m, block]
+        return remote(ref, ref, send.at[m, block, way], recv.at[m, block], (left, right)[way])
+
+    def gather_step(buf, send, recv, m, step):
+        @pl.when(s >= step)
+        def _():
+            block = s - step
+            gather_copy(buf, send, recv, m, block, 1).wait_recv()
+
+            @pl.when(has_right)
+            def _():
+                gather_copy(buf, send, recv, m, block, 1).start()
+
+        @pl.when(s + step < seqs)
+        def _():
+            block = s + step
+            gather_copy(buf, send, recv, m, block, 0).wait_recv()
+
+            @pl.when(has_left)
+            def _():
+                gather_copy(buf, send, recv, m, block, 0).start()
+
+    def gather_own(buf, send, recv, m):
+        @pl.when(has_right)
+        def _():
+            gather_copy(buf, send, recv, m, s, 1).start()
+
+        @pl.when(has_left)
+        def _():
+            gather_copy(buf, send, recv, m, s, 0).start()
+
+    def gather_finish(buf, send, recv):
+        for m in range(users):
+            for block in range(seqs):
+                @pl.when(jnp.logical_and(block <= s, has_right))
+                def _():
+                    gather_copy(buf, send, recv, m, block, 1).wait_send()
+
+                @pl.when(jnp.logical_and(block >= s, has_left))
+                def _():
+                    gather_copy(buf, send, recv, m, block, 0).wait_send()
+
+    loads["cand"].wait()
+    loads["wq"].wait()
+    for m in range(users):
+        queries[m, s] = dot(cand[m], wq[...]).astype(BF16)
+        if m == 0:
+            pl.semaphore_wait(
+                barrier, 3 + has_left.astype(jnp.int32) + has_right.astype(jnp.int32)
+            )
+        gather_own(queries, q_send, q_recv, m)
+    for w in range(2):
+        to_across(w, u).start()
+    for w in range(2):
+        to_partner_own(w, u).start()
+
+    loads["kv"].wait()
+    for m in range(users):
+        slots = s * hist + lax.broadcasted_iota(jnp.int32, (hist, 1), 0)
+        visible = jnp.where(slots < len_ref[m], 1.0, 0.0)
+        values[m] = (kv[m, :, inner:].astype(F32) * visible).astype(BF16)
+
+    half_scale = 0.5 / math.sqrt(DH)
+
+    def attend(m, block):
+        for head in range(HEADS):
+            cols = slice(head * DH, (head + 1) * DH)
+            scores = lax.dot_general(
+                queries[m, block, :, cols], kv[m, :, cols], (((1,), (1,)), ((), ())),
+                preferred_element_type=F32,
+            )
+            weight = silu_of_double(scores * half_scale).astype(BF16)
+            sums[m, block, :, cols] = dot(weight, values[m, :, cols])
+
+    def partial_copy(m, block, way):
+        return remote(
+            outgoing.at[m, block], incoming.at[way, m, block],
+            p_send.at[m, block], p_recv.at[way, m, block], (left, right)[way],
+        )
+
+    def pass_on(m, block, way, first):
+        @pl.when(first)
+        def _():
+            outgoing[m, block] = sums[m, block].astype(BF16)
+
+        @pl.when(jnp.logical_not(first))
+        def _():
+            partial_copy(m, block, way).wait_recv()
+            outgoing[m, block] = (sums[m, block] + incoming[way, m, block].astype(F32)).astype(BF16)
+
+        partial_copy(m, block, way).start()
+
+    mirror = seqs - 1 - s
+    for step in range(max(2 * seqs - 2, seqs)):
+        for m in range(users):
+            if 0 < step < seqs:
+                gather_step(queries, q_send, q_recv, m, step)
+            if step < seqs:
+                @pl.when(s >= step)
+                def _():
+                    attend(m, s - step)
+
+                if step > 0:
+                    @pl.when(s + step < seqs)
+                    def _():
+                        attend(m, s + step)
+
+            block = step - s
+
+            @pl.when(jnp.logical_and(block > s, block < seqs))
+            def _():
+                pass_on(m, block, 1, s == 0)
+
+            far = step - mirror
+
+            @pl.when(jnp.logical_and(far > mirror, far < seqs))
+            def _():
+                pass_on(m, seqs - 1 - far, 0, mirror == 0)
+
+        if step == 0:
+            loads["wg"].wait()
+            for m in range(users):
+                gates[m] = silu_of_double(dot(cand[m], wg[...]) * 0.5)
+        if step == seqs - 1:
+            across_arrived(0)
+
+    for m in range(users):
+        @pl.when(has_left)
+        def _():
+            partial_copy(m, s, 1).wait_recv()
+            sums[m, s] = sums[m, s] + incoming[1, m, s].astype(F32)
+
+        @pl.when(has_right)
+        def _():
+            partial_copy(m, s, 0).wait_recv()
+            sums[m, s] = sums[m, s] + incoming[0, m, s].astype(F32)
+
+        normed[m, s] = layer_norm(sums[m, s]).astype(BF16)
+        gather_own(normed, n_send, n_recv, m)
+    across_arrived(1)
+    for step in range(1, seqs):
+        for m in range(users):
+            gather_step(normed, n_send, n_recv, m, step)
+        if step == 1:
+            group_arrived(0)
+
+    loads["tm"].wait()
+    loads["wo"].wait()
+    ffn_ins = []
+    for m in range(users):
+        mixed = normed[m, s].astype(F32)
+        for block in range(seqs):
+            mixed = mixed + dot(tm[:, block * rows:(block + 1) * rows], normed[m, block])
+        gated = (mixed * gates[m]).astype(BF16)
+        state = cand[m].astype(F32) + dot(gated, wo[...])
+        states[m * rows:(m + 1) * rows] = state
+        ffn_ins.append(layer_norm(state).astype(BF16))
+    ffn_in = jnp.concatenate(ffn_ins, axis=0)
+
+    group_arrived(1)
+    for w in range(2):
+        loads[("wu", "wd")[w]].wait()
+        to_partner_own(w, partner).wait_recv()
+        to_partner_far(w, across_partner, g, 1).wait_recv()
+        to_partner_far(w, across_partner, 1 - g, 2).wait_recv()
+    total = states[...]
+    for slot in range(hidden_slots):
+        hidden = gelu_tanh(dot(ffn_in, wu[slot])).astype(BF16)
+        total = total + dot(hidden, wd[slot])
+    for m in range(users):
+        out_ref[m] = total[m * rows:(m + 1) * rows].astype(BF16)
+
+    gather_finish(queries, q_send, q_recv)
+    gather_finish(normed, n_send, n_recv)
+    for m in range(users):
+        for block in range(seqs):
+            @pl.when(block != s)
+            def _():
+                partial_copy(m, block, 1).wait_send()
+    for w in range(2):
+        to_across(w, u).wait_send()
+        to_partner_own(w, u).wait_send()
+        to_group(w, g).wait_send()
+        to_partner_far(w, across, g, 1).wait_send()
+        to_partner_far(w, across, 1 - g, 2).wait_send()
+
+
+def fused(seqs, usrs, history_kv, candidates, lengths, w_query, w_gate, token_mix, w_out, w_up, w_down):
+    users, hist, _ = history_kv.shape
+    rows, width = candidates.shape[1:]
+    inner = w_query.shape[1]
+    depth = w_up.shape[1]
+    dma = pltpu.SemaphoreType.DMA
+    hbm = pl.BlockSpec(memory_space=pl.ANY)
+    smem = pl.BlockSpec(memory_space=pltpu.SMEM)
+    return pl.pallas_call(
+        functools.partial(kernel, seqs),
+        out_shape=jax.ShapeDtypeStruct(candidates.shape, BF16),
+        in_specs=[hbm, hbm, smem, hbm, hbm, hbm, hbm, hbm, hbm],
+        out_specs=pl.BlockSpec(memory_space=pltpu.VMEM),
+        scratch_shapes=[
+            pltpu.VMEM(history_kv.shape, BF16),
+            pltpu.VMEM(candidates.shape, BF16),
+            pltpu.VMEM(w_query.shape, BF16),
+            pltpu.VMEM(w_gate.shape, BF16),
+            pltpu.VMEM(token_mix.shape, BF16),
+            pltpu.VMEM(w_out.shape, BF16),
+            pltpu.VMEM((usrs, width, depth), BF16),
+            pltpu.VMEM((usrs, depth, width), BF16),
+            pltpu.VMEM((users, hist, inner), BF16),
+            pltpu.VMEM((users, seqs, rows, inner), BF16),
+            pltpu.VMEM((users, seqs, rows, inner), F32),
+            pltpu.VMEM((users, seqs, rows, inner), BF16),
+            pltpu.VMEM((2, users, seqs, rows, inner), BF16),
+            pltpu.VMEM((users, seqs, rows, inner), BF16),
+            pltpu.VMEM((users, rows, inner), F32),
+            pltpu.VMEM((users * rows, width), F32),
+            dma((8,)),
+            dma((users, seqs, 2)), dma((users, seqs)),
+            dma((users, seqs)), dma((2, users, seqs)),
+            dma((users, seqs, 2)), dma((users, seqs)),
+            dma((2, 3)), dma((2, 3)), dma((2,)), dma((2,)), dma((2,)), dma((2,)),
+        ],
+        compiler_params=pltpu.CompilerParams(
+            collective_id=0, has_side_effects=True, vmem_limit_bytes=56 * 1024 * 1024
+        ),
+        name="rank_layer",
+    )(history_kv, candidates, lengths, w_query, w_gate, token_mix, w_out, w_up, w_down)
 
 
 def shards(history_kv, candidates, lengths, w_query, w_gate, token_mix, w_out, w_up, w_down):
@@ -99,8 +428,14 @@
 
 
 def solution(mesh):
+    sizes = dict(mesh.shape)
+    seqs, usrs = sizes["seq"], sizes["usr"]
+    if sizes["grp"] == 2 and usrs == 4 and 2 <= seqs <= 8:
+        body = functools.partial(fused, seqs, usrs)
+    else:
+        body = shards
     return jax.shard_map(
-        shards,
+        body,
         mesh=mesh,
         in_specs=(
             P(("grp", "usr"), "seq", None),

time: 180 us -> 52.9 us (0.29)
  the two profiles are of different devices: /device:TPU:0 before, /device:TPU:1 now
where the time goes in v1:
time: 52.9 us; the launch traced here: 52.8 us
  Pallas kernels  51 us (96%)
  local copies, waits for them, and re-layouts  1.77 us (3%)
    pallas_call x1, Pallas kernels, fused(): pl.pallas_call(functools.partial(kernel, seqs), out_shape=jax.ShapeDtypeS...  51 us
    unnamed x1, local copies, waits for them, and re-layouts  1.77 us

profile of v1, /device:TPU:1, one launch (start us, length us, event | category | flops | bytes accessed | tf_op | source)
XLA Modules:
  0.0 52.8 jit_solution(11228897465234000363)
XLA Ops:
  0.0 51.0 %rank_layer.1 = bf16[2,128,768]{2,1,0:T(8,128)(2,1)} custom-call(bf16[2,512,768]{2,1,0:T(8,128)(2,1)} %kv_hbm.1, bf16[2,128,768]{2,1,0:T(8,128)(2,1)} %cand_hbm.1, s32[2]{0:T(128)} %len_ref.1, bf16[768,384]{1,0:T(8,128)(2,1)} %wq_hbm.1, bf16[768,384]{1,0:T(8,128)(2,1)} %wg_hbm.1, bf16[128,512]{1,0:T(8,128)(2,1)} %tm_hbm.1, bf16[384,768]{1,0:T(8,128)(2,1)} %wo_hbm.1, ...), custom_call_target="tpu_custom_call" | custom-call | tf_op jit(solution)/shard_map/rank_layer/pallas_call | solution.py:312
  51.0 1.8 %copy.11 = bf16[2,128,768]{2,1,0:T(8,128)(2,1)} copy(bf16[2,128,768]{2,1,0:T(8,128)(2,1)} %rank_layer.1) | data formatting | bytes 786432

commit v2 on v1

--- a/solution.py
+++ b/solution.py
@@ -13,6 +13,9 @@
 F32 = jnp.float32
 BF16 = jnp.bfloat16
 MESH = pl.DeviceIdType.MESH
+ACROSS_STEPS = (1, 2, 3, 4)
+GROUP_STEPS = (3, 4, 5, 6)
+MIX_STEP = 2
 
 
 def layer_norm(values):
@@ -38,10 +41,10 @@
     kv_hbm, cand_hbm, len_ref, wq_hbm, wg_hbm, tm_hbm, wo_hbm, wu_hbm, wd_hbm,
     out_ref,
     kv, cand, wq, wg, tm, wo, wu, wd,
-    values, queries, sums, outgoing, incoming, normed, gates, states,
+    values, queries, sums, outgoing, incoming, normed, mixed_out, mixed_in, gates, states,
     load_sem,
-    q_send, q_recv, p_send, p_recv, n_send, n_recv,
-    wc_send, wc_recv, wx_send, wx_recv, wy_send, wy_recv,
+    q_send, q_recv, p_send, p_recv, t_send, t_recv, m_send, m_recv,
+    wo_send, wo_recv, wc_send, wc_recv, wx_send, wx_recv, wy_send, wy_recv,
 ):
     users, rows, _ = cand.shape
     hist = kv.shape[1]
@@ -54,25 +57,23 @@
     left, right = (g, s - 1, u), (g, s + 1, u)
     has_left, has_right = s > 0, s < seqs - 1
 
+    first_owned = lax.rem(u, 2) * users
+    owned = s - first_owned
+    is_owner = jnp.logical_and(owned >= 0, owned < users)
+
     loads = {}
     for index, (name, source, target) in enumerate((
         ("cand", cand_hbm, cand), ("wq", wq_hbm, wq), ("kv", kv_hbm, kv), ("wg", wg_hbm, wg),
-        ("tm", tm_hbm, tm), ("wo", wo_hbm, wo), ("wu", wu_hbm, wu.at[u]), ("wd", wd_hbm, wd.at[u]),
+        ("tm", tm_hbm, tm.at[s]), ("wo", wo_hbm, wo), ("wu", wu_hbm, wu.at[u]), ("wd", wd_hbm, wd.at[u]),
     )):
         loads[name] = pltpu.make_async_copy(source, target, load_sem.at[index])
         loads[name].start()
 
     barrier = pltpu.get_barrier_semaphore()
-    for peer in ((g, s, partner), (g, s, across), (1 - g, s, u)):
+    peers = [(g, s, partner), (g, s, across), (1 - g, s, u)]
+    peers += [(g, lax.rem(s + step, seqs), u) for step in range(1, seqs)]
+    for peer in peers:
         pl.semaphore_signal(barrier, inc=1, device_id=peer, device_id_type=MESH)
-
-    @pl.when(has_left)
-    def _():
-        pl.semaphore_signal(barrier, inc=1, device_id=left, device_id_type=MESH)
-
-    @pl.when(has_right)
-    def _():
-        pl.semaphore_signal(barrier, inc=1, device_id=right, device_id_type=MESH)
 
     def remote(source, target, send, recv, device):
         return pltpu.make_async_remote_copy(
@@ -82,36 +83,36 @@
 
     weights = ((wu_hbm, wu), (wd_hbm, wd))
 
-    def half_of(w, slot, half):
-        size = weights[w][1].shape[1] // 2
-        return weights[w][1].at[slot, pl.ds(pl.multiple_of(half * size, size), size)]
-
-    def own_half(w, half):
-        size = weights[w][1].shape[1] // 2
-        return weights[w][0].at[pl.ds(pl.multiple_of(half * size, size), size)]
+    def rows_of(piece, half):
+        size = weights[piece // 2][1].shape[1] // 4
+        return pl.ds(pl.multiple_of((half * 2 + piece % 2) * size, size), size)
+
+    def piece_of(piece, slot, half):
+        return weights[piece // 2][1].at[slot, rows_of(piece, half)]
 
     def to_partner_own(w, slot):
-        return remote(weights[w][0], weights[w][1].at[slot], wc_send.at[w, 0], wc_recv.at[w, 0], (g, s, partner))
-
-    def to_across(w, slot):
-        return remote(own_half(w, g), half_of(w, slot, g), wx_send.at[w], wx_recv.at[w], (g, s, across))
-
-    def to_group(w, half):
-        part = half_of(w, across, half)
-        return remote(part, part, wy_send.at[w], wy_recv.at[w], (1 - g, s, u))
-
-    def to_partner_far(w, slot, half, which):
-        part = half_of(w, slot, half)
-        return remote(part, part, wc_send.at[w, which], wc_recv.at[w, which], (g, s, partner))
-
-    def across_arrived(w):
-        to_across(w, across).wait_recv()
-        to_group(w, g).start()
-        to_partner_far(w, across, g, 1).start()
-
-    def group_arrived(w):
-        to_group(w, 1 - g).wait_recv()
-        to_partner_far(w, across, 1 - g, 2).start()
+        return remote(weights[w][0], weights[w][1].at[slot], wo_send.at[w], wo_recv.at[w], (g, s, partner))
+
+    def to_across(piece, slot):
+        source = weights[piece // 2][0].at[rows_of(piece, g)]
+        return remote(source, piece_of(piece, slot, g), wx_send.at[piece], wx_recv.at[piece], (g, s, across))
+
+    def to_group(piece, half):
+        part = piece_of(piece, across, half)
+        return remote(part, part, wy_send.at[piece], wy_recv.at[piece], (1 - g, s, u))
+
+    def to_partner_far(piece, slot, half, which):
+        part = piece_of(piece, slot, half)
+        return remote(part, part, wc_send.at[piece, which], wc_recv.at[piece, which], (g, s, partner))
+
+    def across_arrived(piece):
+        to_across(piece, across).wait_recv()
+        to_group(piece, g).start()
+        to_partner_far(piece, across, g, 0).start()
+
+    def group_arrived(piece):
+        to_group(piece, 1 - g).wait_recv()
+        to_partner_far(piece, across, 1 - g, 1).start()
 
     def gather_copy(buf, send, recv, m, block, way):
         ref = buf.at[m, block]
@@ -161,12 +162,10 @@
     for m in range(users):
         queries[m, s] = dot(cand[m], wq[...]).astype(BF16)
         if m == 0:
-            pl.semaphore_wait(
-                barrier, 3 + has_left.astype(jnp.int32) + has_right.astype(jnp.int32)
-            )
+            pl.semaphore_wait(barrier, len(peers))
         gather_own(queries, q_send, q_recv, m)
-    for w in range(2):
-        to_across(w, u).start()
+    for piece in range(4):
+        to_across(piece, u).start()
     for w in range(2):
         to_partner_own(w, u).start()
 
@@ -206,8 +205,11 @@
 
         partial_copy(m, block, way).start()
 
+    def mix_copy(m):
+        return remote(tm_hbm, tm.at[s], t_send.at[m], t_recv.at[s], (g, first_owned + m, u))
+
     mirror = seqs - 1 - s
-    for step in range(max(2 * seqs - 2, seqs)):
+    for step in range(2 * seqs - 2):
         for m in range(users):
             if 0 < step < seqs:
                 gather_step(queries, q_send, q_recv, m, step)
@@ -221,15 +223,16 @@
                     def _():
                         attend(m, s + step)
 
+            owner = first_owned + m
             block = step - s
 
-            @pl.when(jnp.logical_and(block > s, block < seqs))
+            @pl.when((owner > s) & (block >= 0) & (block < seqs))
             def _():
                 pass_on(m, block, 1, s == 0)
 
             far = step - mirror
 
-            @pl.when(jnp.logical_and(far > mirror, far < seqs))
+            @pl.when((owner < s) & (far >= 0) & (far < seqs))
             def _():
                 pass_on(m, seqs - 1 - far, 0, mirror == 0)
 
@@ -237,48 +240,79 @@
             loads["wg"].wait()
             for m in range(users):
                 gates[m] = silu_of_double(dot(cand[m], wg[...]) * 0.5)
-        if step == seqs - 1:
-            across_arrived(0)
-
-    for m in range(users):
-        @pl.when(has_left)
-        def _():
-            partial_copy(m, s, 1).wait_recv()
-            sums[m, s] = sums[m, s] + incoming[1, m, s].astype(F32)
-
-        @pl.when(has_right)
-        def _():
-            partial_copy(m, s, 0).wait_recv()
-            sums[m, s] = sums[m, s] + incoming[0, m, s].astype(F32)
-
-        normed[m, s] = layer_norm(sums[m, s]).astype(BF16)
-        gather_own(normed, n_send, n_recv, m)
-    across_arrived(1)
-    for step in range(1, seqs):
-        for m in range(users):
-            gather_step(normed, n_send, n_recv, m, step)
-        if step == 1:
-            group_arrived(0)
-
+        if step == MIX_STEP:
+            for m in range(users):
+                @pl.when(first_owned + m != s)
+                def _():
+                    mix_copy(m).start()
+        for piece in range(4):
+            if step == ACROSS_STEPS[piece]:
+                across_arrived(piece)
+            if step == GROUP_STEPS[piece]:
+                group_arrived(piece)
+
+    def mixed_copy(block, m):
+        return remote(
+            mixed_out.at[block], mixed_in.at[m], m_send.at[block], m_recv.at[m], (g, block, u)
+        )
+
+    order = sorted(range(seqs), key=lambda block: min(block, seqs - 1 - block))
     loads["tm"].wait()
+
+    @pl.when(is_owner)
+    def _():
+        for block in range(seqs):
+            @pl.when(has_left)
+            def _():
+                partial_copy(owned, block, 1).wait_recv()
+                sums[owned, block] = sums[owned, block] + incoming[1, owned, block].astype(F32)
+
+            @pl.when(has_right)
+            def _():
+                partial_copy(owned, block, 0).wait_recv()
+                sums[owned, block] = sums[owned, block] + incoming[0, owned, block].astype(F32)
+
+            normed[block * rows:(block + 1) * rows] = layer_norm(sums[owned, block]).astype(BF16)
+        for block in range(seqs):
+            @pl.when(block != s)
+            def _():
+                remote(
+                    tm_hbm, tm.at[block], t_send.at[0], t_recv.at[block], (g, lax.rem(s + 1, seqs), u)
+                ).wait_recv()
+        for block in order:
+            mixed = normed[block * rows:(block + 1) * rows].astype(F32) + dot(tm[block], normed[...])
+            mixed_out[block] = mixed.astype(BF16)
+
+            @pl.when(block != s)
+            def _():
+                mixed_copy(block, owned).start()
+
+            @pl.when(block == s)
+            def _():
+                mixed_in[owned] = mixed.astype(BF16)
+
+    for piece in range(4):
+        if GROUP_STEPS[piece] >= 2 * seqs - 2:
+            group_arrived(piece)
     loads["wo"].wait()
     ffn_ins = []
     for m in range(users):
-        mixed = normed[m, s].astype(F32)
-        for block in range(seqs):
-            mixed = mixed + dot(tm[:, block * rows:(block + 1) * rows], normed[m, block])
-        gated = (mixed * gates[m]).astype(BF16)
+        @pl.when(first_owned + m != s)
+        def _():
+            mixed_copy(s, m).wait_recv()
+
+        gated = (mixed_in[m].astype(F32) * gates[m]).astype(BF16)
         state = cand[m].astype(F32) + dot(gated, wo[...])
         states[m * rows:(m + 1) * rows] = state
         ffn_ins.append(layer_norm(state).astype(BF16))
     ffn_in = jnp.concatenate(ffn_ins, axis=0)
 
-    group_arrived(1)
     for w in range(2):
         loads[("wu", "wd")[w]].wait()
         to_partner_own(w, partner).wait_recv()
-        to_partner_far(w, across_partner, g, 1).wait_recv()
-        to_partner_far(w, across_partner, 1 - g, 2).wait_recv()
+    for piece in range(4):
+        to_partner_far(piece, across_partner, g, 0).wait_recv()
+        to_partner_far(piece, across_partner, 1 - g, 1).wait_recv()
     total = states[...]
     for slot in range(hidden_slots):
         hidden = gelu_tanh(dot(ffn_in, wu[slot])).astype(BF16)
@@ -287,18 +321,27 @@
         out_ref[m] = total[m * rows:(m + 1) * rows].astype(BF16)
 
     gather_finish(queries, q_send, q_recv)
-    gather_finish(normed, n_send, n_recv)
     for m in range(users):
+        @pl.when(first_owned + m != s)
+        def _():
+            mix_copy(m).wait_send()
+            for block in range(seqs):
+                partial_copy(m, block, 1).wait_send()
+
+    @pl.when(is_owner)
+    def _():
         for block in range(seqs):
             @pl.when(block != s)
             def _():
-                partial_copy(m, block, 1).wait_send()
+                mixed_copy(block, owned).wait_send()
+
     for w in range(2):
-        to_across(w, u).wait_send()
         to_partner_own(w, u).wait_send()
-        to_group(w, g).wait_send()
-        to_partner_far(w, across, g, 1).wait_send()
-        to_partner_far(w, across, 1 - g, 2).wait_send()
+    for piece in range(4):
+        to_across(piece, u).wait_send()
+        to_group(piece, g).wait_send()
+        to_partner_far(piece, across, g, 0).wait_send()
+        to_partner_far(piece, across, 1 - g, 1).wait_send()
 
 
 def fused(seqs, usrs, history_kv, candidates, lengths, w_query, w_gate, token_mix, w_out, w_up, w_down):
@@ -319,7 +362,7 @@
             pltpu.VMEM(candidates.shape, BF16),
             pltpu.VMEM(w_query.shape, BF16),
             pltpu.VMEM(w_gate.shape, BF16),
-            pltpu.VMEM(token_mix.shape, BF16),
+            pltpu.VMEM((seqs, *token_mix.shape), BF16),
             pltpu.VMEM(w_out.shape, BF16),
             pltpu.VMEM((usrs, width, depth), BF16),
             pltpu.VMEM((usrs, depth, width), BF16),
@@ -328,14 +371,17 @@
             pltpu.VMEM((users, seqs, rows, inner), F32),
             pltpu.VMEM((users, seqs, rows, inner), BF16),
             pltpu.VMEM((2, users, seqs, rows, inner), BF16),
-            pltpu.VMEM((users, seqs, rows, inner), BF16),
+            pltpu.VMEM((seqs * rows, inner), BF16),
+            pltpu.VMEM((seqs, rows, inner), BF16),
+            pltpu.VMEM((users, rows, inner), BF16),
             pltpu.VMEM((users, rows, inner), F32),
             pltpu.VMEM((users * rows, width), F32),
             dma((8,)),
             dma((users, seqs, 2)), dma((users, seqs)),
             dma((users, seqs)), dma((2, users, seqs)),
-            dma((users, seqs, 2)), dma((users, seqs)),
-            dma((2, 3)), dma((2, 3)), dma((2,)), dma((2,)), dma((2,)), dma((2,)),
+            dma((users,)), dma((seqs,)), dma((seqs,)), dma((users,)),
+            dma((2,)), dma((2,)), dma((4, 2)), dma((4, 2)),
+            dma((4,)), dma((4,)), dma((4,)), dma((4,)),
         ],
         compiler_params=pltpu.CompilerParams(
             collective_id=0, has_side_effects=True, vmem_limit_bytes=56 * 1024 * 1024
@@ -430,10 +476,12 @@
 def solution(mesh):
     sizes = dict(mesh.shape)
     seqs, usrs = sizes["seq"], sizes["usr"]
-    if sizes["grp"] == 2 and usrs == 4 and 2 <= seqs <= 8:
-        body = functools.partial(fused, seqs, usrs)
-    else:
-        body = shards
+    def body(history_kv, candidates, *rest):
+        operands = (history_kv, candidates, *rest)
+        if sizes["grp"] == 2 and usrs == 4 and seqs == 2 * candidates.shape[0] and seqs >= 4:
+            return fused(seqs, usrs, *operands)
+        return shards(*operands)
+
     return jax.shard_map(
         body,
         mesh=mesh,

time: 52.9 us -> 48.9 us (0.924)
  the two profiles are of different devices: /device:TPU:1 before, /device:TPU:20 now
where the time goes in v2:
time: 48.9 us; the launch traced here: 48.7 us
  Pallas kernels  47 us (96%)
  local copies, waits for them, and re-layouts  1.77 us (4%)
    pallas_call x1, Pallas kernels, fused(): pl.pallas_call(functools.partial(kernel, seqs), out_shape=jax.ShapeDtypeS...  47 us
    unnamed x1, local copies, waits for them, and re-layouts  1.77 us

profile of v2, /device:TPU:20, one launch (start us, length us, event | category | flops | bytes accessed | tf_op | source)
XLA Modules:
  0.0 48.7 jit_solution(11804613022881251790)
XLA Ops:
  0.0 47.0 %rank_layer.1 = bf16[2,128,768]{2,1,0:T(8,128)(2,1)} custom-call(bf16[2,512,768]{2,1,0:T(8,128)(2,1)} %kv_hbm.1, bf16[2,128,768]{2,1,0:T(8,128)(2,1)} %cand_hbm.1, s32[2]{0:T(128)} %len_ref.1, bf16[768,384]{1,0:T(8,128)(2,1)} %wq_hbm.1, bf16[768,384]{1,0:T(8,128)(2,1)} %wg_hbm.1, bf16[128,512]{1,0:T(8,128)(2,1)} %tm_hbm.1, bf16[384,768]{1,0:T(8,128)(2,1)} %wo_hbm.1, ...), custom_call_target="tpu_custom_call" | custom-call | tf_op jit(solution)/shard_map/rank_layer/pallas_call | solution.py:355
  47.0 1.8 %copy.11 = bf16[2,128,768]{2,1,0:T(8,128)(2,1)} copy(bf16[2,128,768]{2,1,0:T(8,128)(2,1)} %rank_layer.1) | data formatting | bytes 786432

commit v3 on v2

--- a/solution.py
+++ b/solution.py
@@ -15,7 +15,8 @@
 MESH = pl.DeviceIdType.MESH
 ACROSS_STEPS = (1, 2, 3, 4)
 GROUP_STEPS = (3, 4, 5, 6)
-MIX_STEP = 2
+MIX_STEP = 0
+SHARE_STEPS = (3, 4)
 
 
 def layer_norm(values):
@@ -43,7 +44,7 @@
     kv, cand, wq, wg, tm, wo, wu, wd,
     values, queries, sums, outgoing, incoming, normed, mixed_out, mixed_in, gates, states,
     load_sem,
-    q_send, q_recv, p_send, p_recv, t_send, t_recv, m_send, m_recv,
+    q_send, q_recv, p_send, p_recv, t_send, t_recv, f_send, m_send, m_recv,
     wo_send, wo_recv, wc_send, wc_recv, wx_send, wx_recv, wy_send, wy_recv,
 ):
     users, rows, _ = cand.shape
@@ -67,6 +68,8 @@
         ("tm", tm_hbm, tm.at[s]), ("wo", wo_hbm, wo), ("wu", wu_hbm, wu.at[u]), ("wd", wd_hbm, wd.at[u]),
     )):
         loads[name] = pltpu.make_async_copy(source, target, load_sem.at[index])
+
+    for name in ("cand", "wq"):
         loads[name].start()
 
     barrier = pltpu.get_barrier_semaphore()
@@ -166,6 +169,8 @@
         gather_own(queries, q_send, q_recv, m)
     for piece in range(4):
         to_across(piece, u).start()
+    for name in ("kv", "wg", "tm", "wo", "wu", "wd"):
+        loads[name].start()
     for w in range(2):
         to_partner_own(w, u).start()
 
@@ -205,36 +210,81 @@
 
         partial_copy(m, block, way).start()
 
+    chip = lax.div(u, 2)
+    quarter = rows // 4
+
+    def quarter_rows(group, near):
+        return pl.ds(pl.multiple_of((group * 2 + near) * quarter, quarter), quarter)
+
     def mix_copy(m):
-        return remote(tm_hbm, tm.at[s], t_send.at[m], t_recv.at[s], (g, first_owned + m, u))
+        return remote(
+            tm_hbm.at[quarter_rows(g, chip)], tm.at[s, quarter_rows(g, chip)],
+            t_send.at[m], t_recv.at[s, 0], (g, first_owned + m, u),
+        )
+
+    def mix_share(block, which):
+        part = tm.at[block, quarter_rows(g, 1 - chip if which == 3 else chip)]
+        device = (g, s, across) if which == 1 else (1 - g, s, u)
+        return remote(part, part, f_send.at[block, which], t_recv.at[block, which], device)
+
+    def mix_arrived(block, which):
+        part = tm.at[block, quarter_rows(1 - g if which > 1 else g, 1 - chip if which % 2 else chip)]
+        remote(part, part, f_send.at[block, which], t_recv.at[block, which], (1 - g, s, u)).wait_recv()
+
+    def for_far_blocks(do):
+        for block in range(seqs):
+            @pl.when(jnp.logical_and(is_owner, block != s))
+            def _():
+                do(block)
+
+    def share_first(block):
+        mix_arrived(block, 0)
+        mix_share(block, 1).start()
+        mix_share(block, 2).start()
+
+    def share_second(block):
+        mix_arrived(block, 1)
+        mix_share(block, 3).start()
+
+    def share_last(block):
+        mix_arrived(block, 2)
+        mix_arrived(block, 3)
+
+    def share_sent(block):
+        for which in (1, 2, 3):
+            mix_share(block, which).wait_send()
 
     mirror = seqs - 1 - s
+    def stage_of(step, m):
+        if step < seqs:
+            if step > 0:
+                gather_step(queries, q_send, q_recv, m, step)
+
+            @pl.when(s >= step)
+            def _():
+                attend(m, s - step)
+
+            if step > 0:
+                @pl.when(s + step < seqs)
+                def _():
+                    attend(m, s + step)
+
+        owner = first_owned + m
+        block = step - s
+
+        @pl.when((owner > s) & (block >= 0) & (block < seqs))
+        def _():
+            pass_on(m, block, 1, s == 0)
+
+        far = step - mirror
+
+        @pl.when((owner < s) & (far >= 0) & (far < seqs))
+        def _():
+            pass_on(m, seqs - 1 - far, 0, mirror == 0)
+
     for step in range(2 * seqs - 2):
         for m in range(users):
-            if 0 < step < seqs:
-                gather_step(queries, q_send, q_recv, m, step)
-            if step < seqs:
-                @pl.when(s >= step)
-                def _():
-                    attend(m, s - step)
-
-                if step > 0:
-                    @pl.when(s + step < seqs)
-                    def _():
-                        attend(m, s + step)
-
-            owner = first_owned + m
-            block = step - s
-
-            @pl.when((owner > s) & (block >= 0) & (block < seqs))
-            def _():
-                pass_on(m, block, 1, s == 0)
-
-            far = step - mirror
-
-            @pl.when((owner < s) & (far >= 0) & (far < seqs))
-            def _():
-                pass_on(m, seqs - 1 - far, 0, mirror == 0)
+            stage_of(step, m)
 
         if step == 0:
             loads["wg"].wait()
@@ -245,6 +295,10 @@
                 @pl.when(first_owned + m != s)
                 def _():
                     mix_copy(m).start()
+        if step == SHARE_STEPS[0]:
+            for_far_blocks(share_first)
+        if step == SHARE_STEPS[1]:
+            for_far_blocks(share_second)
         for piece in range(4):
             if step == ACROSS_STEPS[piece]:
                 across_arrived(piece)
@@ -258,6 +312,7 @@
 
     order = sorted(range(seqs), key=lambda block: min(block, seqs - 1 - block))
     loads["tm"].wait()
+    for_far_blocks(share_last)
 
     @pl.when(is_owner)
     def _():
@@ -273,12 +328,6 @@
                 sums[owned, block] = sums[owned, block] + incoming[0, owned, block].astype(F32)
 
             normed[block * rows:(block + 1) * rows] = layer_norm(sums[owned, block]).astype(BF16)
-        for block in range(seqs):
-            @pl.when(block != s)
-            def _():
-                remote(
-                    tm_hbm, tm.at[block], t_send.at[0], t_recv.at[block], (g, lax.rem(s + 1, seqs), u)
-                ).wait_recv()
         for block in order:
             mixed = normed[block * rows:(block + 1) * rows].astype(F32) + dot(tm[block], normed[...])
             mixed_out[block] = mixed.astype(BF16)
@@ -321,6 +370,7 @@
         out_ref[m] = total[m * rows:(m + 1) * rows].astype(BF16)
 
     gather_finish(queries, q_send, q_recv)
+    for_far_blocks(share_sent)
     for m in range(users):
         @pl.when(first_owned + m != s)
         def _():
@@ -379,7 +429,7 @@
             dma((8,)),
             dma((users, seqs, 2)), dma((users, seqs)),
             dma((users, seqs)), dma((2, users, seqs)),
-            dma((users,)), dma((seqs,)), dma((seqs,)), dma((users,)),
+            dma((users,)), dma((seqs, 4)), dma((seqs, 4)), dma((seqs,)), dma((users,)),
             dma((2,)), dma((2,)), dma((4, 2)), dma((4, 2)),
             dma((4,)), dma((4,)), dma((4,)), dma((4,)),
         ],

time: 48.9 us -> 45.4 us (0.928)
  the two profiles are of different devices: /device:TPU:20 before, /device:TPU:0 now
where the time goes in v3:
time: 45.4 us; the launch traced here: 45.3 us
  Pallas kernels  43.5 us (96%)
  local copies, waits for them, and re-layouts  1.77 us (4%)
    pallas_call x1, Pallas kernels, fused(): pl.pallas_call(functools.partial(kernel, seqs), out_shape=jax.ShapeDtypeS...  43.5 us
    unnamed x1, local copies, waits for them, and re-layouts  1.77 us

profile of v3, /device:TPU:0, one launch (start us, length us, event | category | flops | bytes accessed | tf_op | source)
XLA Modules:
  0.0 45.3 jit_solution(4290668322616653034)
XLA Ops:
  0.0 43.5 %rank_layer.1 = bf16[2,128,768]{2,1,0:T(8,128)(2,1)} custom-call(bf16[2,512,768]{2,1,0:T(8,128)(2,1)} %kv_hbm.1, bf16[2,128,768]{2,1,0:T(8,128)(2,1)} %cand_hbm.1, s32[2]{0:T(128)} %len_ref.1, bf16[768,384]{1,0:T(8,128)(2,1)} %wq_hbm.1, bf16[768,384]{1,0:T(8,128)(2,1)} %wg_hbm.1, bf16[128,512]{1,0:T(8,128)(2,1)} %tm_hbm.1, bf16[384,768]{1,0:T(8,128)(2,1)} %wo_hbm.1, ...), custom_call_target="tpu_custom_call" | custom-call | tf_op jit(solution)/shard_map/rank_layer/pallas_call | solution.py:405
  43.5 1.8 %copy.11 = bf16[2,128,768]{2,1,0:T(8,128)(2,1)} copy(bf16[2,128,768]{2,1,0:T(8,128)(2,1)} %rank_layer.1) | data formatting | bytes 786432
